TPU v7x, 32 devices: a whole 2x2x4 slice. The times are simulated.
32 devices in a mesh: grp: 2 (over x), tok: 16 (over z, y, core).
Axes of the slice: x: 2, y: 2, z: 4, core: 2. Of those that a mesh axis runs over, the one named last changes fastest.
Arguments:
- keys: bfloat16 [4096, 1024], P(('grp', 'tok')), parts along dimension 0, may hold values from -6 to 6
- values: bfloat16 [4096, 1024], P(('grp', 'tok')), parts along dimension 0, may hold values from -6 to 6
- queries: bfloat16 [4096, 1024], P(('grp', 'tok')), parts along dimension 0, may hold values from -6 to 6
- rates: float32 [2, 4096], P(None, ('grp', 'tok')), parts along dimension 1, may hold values from 0.3 to 3
- fast_weights: bfloat16 [2, 3, 512, 512], replicated, may hold values from -0.25 to 0.25
Outputs:
- readout: bfloat16 [4096, 1024], P(('grp', 'tok')), parts along dimension 0
- new_weights: bfloat16 [4, 3, 512, 512], P('grp'), parts along dimension 0
There are 2 independent parts, one for each index of `grp`. A program takes and returns all parts, laid end to end along the dimension named above; an argument that names none is the same for every part. Nothing has to cross between parts.
All inputs are finite; a program needn't handle non-finite values.
Results may differ from a plain program's by a relative error of at most 0.017.
Values may be sent and summed in bfloat16 or wider, within the bound.
A program may use at most 64 MiB of HBM per device.

v0:
```python
import jax
import jax.numpy as jnp
from jax import lax
from jax.sharding import PartitionSpec as P

DH = 512
HEADS = 2
NS_STEPS = 2


def swiglu_grads(key_rows, value_rows, rate_col, gate_w, up_w, down_w):
    gate = jnp.dot(key_rows, gate_w, preferred_element_type=jnp.float32)
    upper = jnp.dot(key_rows, up_w, preferred_element_type=jnp.float32)
    sigma = jax.nn.sigmoid(gate)
    silu_gate = gate * sigma
    hidden = (silu_gate * upper).astype(jnp.bfloat16)
    outer = (-rate_col[:, None] * value_rows.astype(jnp.float32)).astype(jnp.bfloat16)
    back = jnp.dot(outer, down_w.T, preferred_element_type=jnp.float32)
    d_gate = (back * upper * sigma * (1.0 + gate * (1.0 - sigma))).astype(jnp.bfloat16)
    d_upper = (back * silu_gate).astype(jnp.bfloat16)
    grad_gate = jnp.dot(key_rows.T, d_gate, preferred_element_type=jnp.float32)
    grad_upper = jnp.dot(key_rows.T, d_upper, preferred_element_type=jnp.float32)
    grad_down = jnp.dot(hidden.T, outer, preferred_element_type=jnp.float32)
    return jnp.stack([grad_gate, grad_upper, grad_down])


def newton_schulz(matrix):
    wide = matrix.astype(jnp.float32)
    iterate = (wide / (jnp.sqrt(jnp.sum(wide * wide)) + 1e-07)).astype(jnp.bfloat16)
    for step in range(NS_STEPS):
        gram = jnp.dot(iterate, iterate.T, preferred_element_type=jnp.float32).astype(jnp.bfloat16)
        square = jnp.dot(gram, gram, preferred_element_type=jnp.float32)
        mixed = (-4.775 * gram.astype(jnp.float32) + 2.0315 * square).astype(jnp.bfloat16)
        iterate = (
            3.4445 * iterate.astype(jnp.float32)
            + jnp.dot(mixed, iterate, preferred_element_type=jnp.float32)
        ).astype(jnp.bfloat16)
    return iterate


def renormed(weight, update):
    old = weight.astype(jnp.float32)
    fresh = old - update.astype(jnp.float32)
    scale = jnp.sqrt(
        (jnp.mean(old * old, axis=1, keepdims=True) + 1e-06)
        / (jnp.mean(fresh * fresh, axis=1, keepdims=True) + 1e-06)
    )
    return (fresh * scale).astype(jnp.bfloat16)


def apply_fast(query_rows, gate_w, up_w, down_w):
    gate = jnp.dot(query_rows, gate_w, preferred_element_type=jnp.float32)
    upper = jnp.dot(query_rows, up_w, preferred_element_type=jnp.float32)
    hidden = (jax.nn.silu(gate) * upper).astype(jnp.bfloat16)
    return jnp.dot(hidden, down_w, preferred_element_type=jnp.float32).astype(jnp.bfloat16)


def summed_grads(partial_value):
    total = lax.psum(partial_value, "tok")
    return total.astype(jnp.bfloat16)


def body(keys, values, queries, rates, fast_weights):
    width = fast_weights.shape[2]
    count = 3 * HEADS
    rounded_all = []
    for head in range(HEADS):
        cols = slice(head * DH, (head + 1) * DH)
        partial_value = swiglu_grads(
            keys[:, cols],
            values[:, cols],
            rates[head],
            fast_weights[head, 0],
            fast_weights[head, 1],
            fast_weights[head, 2],
        )
        rounded_all.append(summed_grads(partial_value))
    stacked = jnp.concatenate(rounded_all, axis=0)
    old_all = fast_weights.reshape(count, width, width)
    fresh_all = [
        renormed(old_all[matrix], newton_schulz(stacked[matrix])) for matrix in range(count)
    ]
    outputs = []
    for head in range(HEADS):
        cols = slice(head * DH, (head + 1) * DH)
        outputs.append(
            apply_fast(
                queries[:, cols],
                fresh_all[3 * head],
                fresh_all[3 * head + 1],
                fresh_all[3 * head + 2],
            )
        )
    new_weights = jnp.stack(fresh_all).reshape(HEADS, 3, width, width)
    return (jnp.concatenate(outputs, axis=1), new_weights)


def solution(mesh):
    return jax.shard_map(
        body,
        mesh=mesh,
        in_specs=(
            P(("grp", "tok"), None),
            P(("grp", "tok"), None),
            P(("grp", "tok"), None),
            P(None, ("grp", "tok")),
            P(),
        ),
        out_specs=(P(("grp", "tok"), None), P("grp", None, None, None)),
        check_vma=False,
    )
```

profile of v0, /device:TPU:11, one launch (start us, length us, event | category | flops | bytes accessed | tf_op | source)
XLA Modules:
  0.0 253.9 jit_solution(15024841520664925883)
XLA Ops:
  1.5 1.6 fusion.100
  8.9 2.0 pad_maximum_fusion.1
  12.0 2.0 pad_maximum_fusion
  14.0 142.8 %all-reduce.2 = (bf16[3,512,512]{1,2,0:T(8,128)(2,1)}, bf16[3,512,512]{1,2,0:T(8,128)(2,1)}) all-reduce(f32[3,512,512]{1,2,0:T(8,128)} %pad_maximum_fusion.1, f32[3,512,512]{1,2,0:T(8,128)} %pad_maximum_fusion), channel_id=1, replica_groups=mesh['grp'=2,'tok'=16] {'tok'}, use_global_device_ids=true, to_apply=%region_10.0 | all-reduce | flops 1572864 | bytes 9437184 | tf_op jit(solution)/shard_map/psum | solution.py:59
  156.8 3.1 %fusion.50 = (f32[]{:T(128)}, f32[]{:T(128)}, f32[]{:T(128)}, f32[]{:T(128)}, f32[]{:T(128)}, /*index=5*/f32[]{:T(128)}) fusion(bf16[3,512,512]{1,2,0:T(8,128)(2,1)} %get-tuple-element.17, bf16[3,512,512]{1,2,0:T(8,128)(2,1)} %get-tuple-element.16), kind=kLoop, calls=%fused_computation.124 | loop fusion | flops 4718586 | bytes 3145752 | tf_op jit(solution)/shard_map/reduce_sum | solution.py:29
  164.0 2.6 %convolution_convert_fusion.7 = bf16[512,512]{1,0:T(8,128)(2,1)} fusion(f32[]{:T(128)S(6)} %add.226, bf16[3,512,512]{1,2,0:T(8,128)(2,1)} %get-tuple-element.17), kind=kOutput, calls=%fused_computation.87 | convolution fusion | flops 269484032 | bytes 1048580 | tf_op jit(solution)/shard_map/dot_general | solution.py:31
  166.6 3.5 %fusion.30 = bf16[512,512]{0,1:T(8,128)(2,1)} fusion(bf16[512,512]{1,0:T(8,128)(2,1)} %convolution_convert_fusion.7, f32[]{:T(128)S(6)} %add.226, bf16[3,512,512]{1,2,0:T(8,128)(2,1)} %get-tuple-element.17), kind=kOutput, calls=%fused_computation.98 | convolution fusion | flops 540803072 | bytes 3146752 | tf_op jit(solution)/shard_map/dot_general | solution.py:36
  170.1 2.5 convolution_convert_fusion.6
  172.6 2.5 convolution_convert_fusion.9
  175.1 3.5 %fusion.27 = bf16[512,512]{0,1:T(8,128)(2,1)} fusion(bf16[512,512]{1,0:T(8,128)(2,1)} %convolution_convert_fusion.9, f32[]{:T(128)S(6)} %add.219, bf16[3,512,512]{1,2,0:T(8,128)(2,1)} %get-tuple-element.17), kind=kOutput, calls=%fused_computation.95 | convolution fusion | flops 540803072 | bytes 3146752 | tf_op jit(solution)/shard_map/dot_general | solution.py:36
  178.5 2.5 convolution_convert_fusion.8
  181.0 2.5 convolution_convert_fusion.11
  183.5 3.5 %fusion.24 = bf16[512,512]{0,1:T(8,128)(2,1)} fusion(bf16[512,512]{1,0:T(8,128)(2,1)} %convolution_convert_fusion.11, f32[]{:T(128)S(6)} %add.211, bf16[3,512,512]{1,2,0:T(8,128)(2,1)} %get-tuple-element.17), kind=kOutput, calls=%fused_computation.92 | convolution fusion | flops 540803072 | bytes 3146752 | tf_op jit(solution)/shard_map/dot_general | solution.py:36
  186.9 2.5 convolution_convert_fusion.10
  189.4 2.5 convolution_convert_fusion.5
  191.9 3.5 %fusion.33 = bf16[512,512]{0,1:T(8,128)(2,1)} fusion(bf16[512,512]{1,0:T(8,128)(2,1)} %convolution_convert_fusion.5, f32[]{:T(128)S(6)} %add.235, bf16[3,512,512]{1,2,0:T(8,128)(2,1)} %get-tuple-element.16), kind=kOutput, calls=%fused_computation.101 | convolution fusion | flops 540803072 | bytes 3146752 | tf_op jit(solution)/shard_map/dot_general | solution.py:36
  195.4 2.5 convolution_convert_fusion.4
  197.9 2.5 convolution_convert_fusion.3
  200.4 3.6 %fusion.36 = bf16[512,512]{0,1:T(8,128)(2,1)} fusion(bf16[512,512]{1,0:T(8,128)(2,1)} %convolution_convert_fusion.3, f32[]{:T(128)S(6)} %add.243, bf16[3,512,512]{1,2,0:T(8,128)(2,1)} %get-tuple-element.16), kind=kOutput, calls=%fused_computation.104 | convolution fusion | flops 540803072 | bytes 3146752 | tf_op jit(solution)/shard_map/dot_general | solution.py:36
  204.0 2.6 %convolution_convert_fusion.2 = bf16[512,512]{1,0:T(8,128)(2,1)} fusion(bf16[512,512]{0,1:T(8,128)(2,1)} %fusion.36), kind=kOutput, calls=%fused_computation.82 | convolution fusion | flops 268697600 | bytes 1048576 | tf_op jit(solution)/shard_map/dot_general | solution.py:31
  206.5 2.5 convolution_convert_fusion.1
  209.0 3.4 %fusion.39 = bf16[512,512]{0,1:T(8,128)(2,1)} fusion(bf16[512,512]{1,0:T(8,128)(2,1)} %convolution_convert_fusion.1, f32[]{:T(128)S(6)} %add.250, bf16[3,512,512]{1,2,0:T(8,128)(2,1)} %get-tuple-element.16), kind=kOutput, calls=%fused_computation.107 | convolution fusion | flops 540803072 | bytes 3146752 | tf_op jit(solution)/shard_map/dot_general | solution.py:36
  212.4 2.5 convolution_convert_fusion
  214.9 2.8 %copy.7 = bf16[2,3,512,512]{2,3,1,0:T(8,128)(2,1)} copy(bf16[2,3,512,512]{3,2,1,0:T(8,128)(2,1)S(1)} %copy-done) | data formatting | bytes 6291456 | tf_op args[4]
  217.7 3.8 %multiply_reduce_fusion = (f32[512]{0:T(512)S(1)}, f32[512,512]{0,1:T(8,128)}) fusion(bf16[512,512]{0,1:T(8,128)(2,1)} %fusion.39, bf16[512,512]{1,0:T(8,128)(2,1)} %convolution_convert_fusion, bf16[6,512,512]{1,2,0:T(8,128)(2,1)} %bitcast.202), kind=kOutput, calls=%fused_computation.139 | convolution fusion | flops 540540416 | bytes 4196352 | tf_op jit(solution)/shard_map/dot_general | solution.py:36
  221.5 3.6 %multiply_reduce_fusion.1 = (f32[512]{0:T(512)S(1)}, f32[512,512]{0,1:T(8,128)}) fusion(bf16[512,512]{0,1:T(8,128)(2,1)} %fusion.36, bf16[512,512]{1,0:T(8,128)(2,1)} %convolution_convert_fusion.2, bf16[6,512,512]{1,2,0:T(8,128)(2,1)S(1)} %bitcast.203), kind=kOutput, calls=%fused_computation.145 | convolution fusion | flops 540540416 | bytes 4196352 | tf_op jit(solution)/shard_map/dot_general | solution.py:36
  225.1 3.6 %multiply_reduce_fusion.2 = (f32[512]{0:T(512)S(1)}, f32[512,512]{0,1:T(8,128)}) fusion(bf16[512,512]{0,1:T(8,128)(2,1)} %fusion.33, bf16[512,512]{1,0:T(8,128)(2,1)} %convolution_convert_fusion.4, bf16[6,512,512]{1,2,0:T(8,128)(2,1)S(1)} %bitcast.204), kind=kOutput, calls=%fused_computation.151 | convolution fusion | flops 540540416 | bytes 4196352 | tf_op jit(solution)/shard_map/dot_general | solution.py:36
  228.7 3.6 %multiply_reduce_fusion.3 = (f32[512]{0:T(512)S(1)}, f32[512,512]{0,1:T(8,128)}) fusion(bf16[512,512]{0,1:T(8,128)(2,1)} %fusion.30, bf16[512,512]{1,0:T(8,128)(2,1)} %convolution_convert_fusion.6, bf16[6,512,512]{1,2,0:T(8,128)(2,1)S(1)} %bitcast.205), kind=kOutput, calls=%fused_computation.157 | convolution fusion | flops 540540416 | bytes 4196352 | tf_op jit(solution)/shard_map/dot_general | solution.py:36
  232.3 3.7 %multiply_reduce_fusion.4 = (f32[512]{0:T(512)S(1)}, f32[512,512]{0,1:T(8,128)}) fusion(bf16[512,512]{0,1:T(8,128)(2,1)} %fusion.27, bf16[512,512]{1,0:T(8,128)(2,1)} %convolution_convert_fusion.8, bf16[6,512,512]{1,2,0:T(8,128)(2,1)S(1)} %bitcast.206), kind=kOutput, calls=%fused_computation.163 | convolution fusion | flops 540540416 | bytes 4196352 | tf_op jit(solution)/shard_map/dot_general | solution.py:36
  236.0 3.8 %multiply_reduce_fusion.5 = (f32[512]{0:T(512)S(1)}, f32[512,512]{0,1:T(8,128)}) fusion(bf16[512,512]{0,1:T(8,128)(2,1)} %fusion.24, bf16[512,512]{1,0:T(8,128)(2,1)} %convolution_convert_fusion.10, bf16[6,512,512]{1,2,0:T(8,128)(2,1)S(1)} %bitcast.207), kind=kOutput, calls=%fused_computation.169 | convolution fusion | flops 540540416 | bytes 4196352 | tf_op jit(solution)/shard_map/dot_general | solution.py:36
  242.0 2.1 convolution_convert_fusion.12
  251.1 2.8 %copy.12 = bf16[2,3,512,512]{3,2,1,0:T(8,128)(2,1)} copy(bf16[2,3,512,512]{2,3,1,0:T(8,128)(2,1)S(1)} %bitcast.209) | data formatting | bytes 6291456
  (57 shorter events, 16.7 us)
Async XLA Ops:
  0.6 6.7 %copy-start.10 = (bf16[128,1024]{1,0:T(8,128)(2,1)S(1)}, bf16[128,1024]{1,0:T(8,128)(2,1)}, u32[]{:S(2)}) copy-start(bf16[128,1024]{1,0:T(8,128)(2,1)} %param.5) | copy-start | bytes 786436
  0.6 6.7 %copy-start = (bf16[2,3,512,512]{3,2,1,0:T(8,128)(2,1)S(1)}, bf16[2,3,512,512]{3,2,1,0:T(8,128)(2,1)}, u32[]{:S(2)}) copy-start(bf16[2,3,512,512]{3,2,1,0:T(8,128)(2,1)} %param.9) | copy-start | bytes 9437188
  0.7 7.1 %copy-start.11 = (bf16[128,1024]{1,0:T(8,128)(2,1)S(1)}, bf16[128,1024]{1,0:T(8,128)(2,1)}, u32[]{:S(2)}) copy-start(bf16[128,1024]{1,0:T(8,128)(2,1)} %param.6) | copy-start | bytes 786436
  217.7 3.8 %copy-start.1 = (bf16[2,3,512,512]{2,3,1,0:T(8,128)(2,1)S(1)}, bf16[2,3,512,512]{2,3,1,0:T(8,128)(2,1)}, u32[]{:S(2)}) copy-start(bf16[2,3,512,512]{2,3,1,0:T(8,128)(2,1)} %copy.7) | copy-start | bytes 9437188
  239.7 2.0 copy-start.7
  239.8 2.0 copy-start.12
  240.4 3.8 %copy-start.9 = (f32[512,512]{0,1:T(8,128)S(1)}, f32[512,512]{0,1:T(8,128)}, u32[]{:S(2)}) copy-start(f32[512,512]{0,1:T(8,128)} %get-tuple-element.27) | copy-start | bytes 3145732
  240.4 5.0 %copy-start.4 = (f32[512,512]{0,1:T(8,128)S(1)}, f32[512,512]{0,1:T(8,128)}, u32[]{:S(2)}) copy-start(f32[512,512]{0,1:T(8,128)} %get-tuple-element.31) | copy-start | bytes 3145732
  240.4 5.0 %copy-start.6 = (f32[512,512]{0,1:T(8,128)S(1)}, f32[512,512]{0,1:T(8,128)}, u32[]{:S(2)}) copy-start(f32[512,512]{0,1:T(8,128)} %get-tuple-element.29) | copy-start | bytes 3145732
  246.9 3.7 %copy-start.5 = (f32[512,512]{0,1:T(8,128)S(1)}, f32[512,512]{0,1:T(8,128)}, u32[]{:S(2)}) copy-start(f32[512,512]{0,1:T(8,128)} %get-tuple-element.31) | copy-start | bytes 3145732
  246.9 3.7 %copy-start.13 = (f32[512]{0:T(512)S(1)}, f32[512]{0:T(512)}, u32[]{:S(2)}) copy-start(f32[512]{0:T(512)} %fusion.172) | copy-start | bytes 6148
  246.9 3.8 %copy-start.8 = (f32[512,512]{0,1:T(8,128)S(1)}, f32[512,512]{0,1:T(8,128)}, u32[]{:S(2)}) copy-start(f32[512,512]{0,1:T(8,128)} %get-tuple-element.21) | copy-start | bytes 3145732
  247.7 3.2 %copy-start.3 = (f32[512,512]{0,1:T(8,128)S(1)}, f32[512,512]{0,1:T(8,128)}, u32[]{:S(2)}) copy-start(f32[512,512]{0,1:T(8,128)} %get-tuple-element.23) | copy-start | bytes 3145732
  249.1 1.9 copy-start.2
where the time goes:
time: 255 us; the launch traced here: 254 us
  blocking collectives  143 us (56%)
  matrix products  86.6 us (34%)
  other arithmetic  13.9 us (5%)
  local copies, waits for them, and re-layouts  5.62 us (2%)
  between operations  5.04 us (2%)
    psum x1, blocking collectives, summed_grads(): total = lax.psum(partial_value, 'tok')  143 us
    dot_general x12, matrix products, newton_schulz(): jnp.dot(mixed, iterate, preferred_element_type=jnp.float32)  43 us
    dot_general x12, matrix products, newton_schulz(): jnp.dot(iterate, iterate.T, preferred_element_type=jnp.float32)  30 us
    unnamed x30, local copies, waits for them, and re-layouts  5.62 us

commit v1 on v0

--- a/solution.py
+++ b/solution.py
@@ -56,7 +56,9 @@
 
 
 def summed_grads(partial_value):
-    total = lax.psum(partial_value, "tok")
+    total = partial_value
+    for hop in (1, 2, 4, 8):
+        total = total + lax.ppermute(total, "tok", [(dev, dev ^ hop) for dev in range(16)])
     return total.astype(jnp.bfloat16)
 
 

time: 255 us -> 519 us (2.04); the launches traced: 254 us -> 512 us
  waiting for transfers between devices: 0 us -> 373 us
  blocking collectives: 143 us -> 0 us
  other arithmetic: 13.9 us -> 27.3 us
  starting transfers between devices: 0 us -> 10.1 us
    ppermute x0 -> x8, waiting for transfers between devices: none -> 373 us  [summed_grads(): lax.ppermute(total, 'tok', [(dev, dev ^ hop) for dev in range(16)])]
    psum x1 -> x0, blocking collectives: 143 us -> none  [summed_grads(): total = lax.psum(partial_value, 'tok')]
    ppermute x0 -> x8, starting transfers between devices: none -> 10.1 us  [summed_grads(): lax.ppermute(total, 'tok', [(dev, dev ^ hop) for dev in range(16)])]
    add x0 -> x6, other arithmetic: none -> 8.65 us  [summed_grads(): total + lax.ppermute(total, 'tok', [(dev, dev ^ hop) for dev in range(16)])]
    convert_element_type x0 -> x2, other arithmetic: none -> 6.76 us  [summed_grads(): return total.astype(jnp.bfloat16)]
  transfers between devices with their start and end apart: 0 -> 8, of which waited for: 0 -> 7; matrix products, arithmetic and copies ran while one was open for 0% -> 6% of each run, Pallas kernels for 0% -> 0%
where the time goes in v1:
time: 519 us; the launch traced here: 512 us
  waiting for transfers between devices  373 us (72%)
  matrix products  88.5 us (17%)
  other arithmetic  27.3 us (5%)
  starting transfers between devices  10.1 us (2%)
  local copies, waits for them, and re-layouts  7.63 us (1%)
    ppermute x8, waiting for transfers between devices, summed_grads(): lax.ppermute(total, 'tok', [(dev, dev ^ hop) for dev in range(16)])  373 us
    dot_general x12, matrix products, newton_schulz(): jnp.dot(mixed, iterate, preferred_element_type=jnp.float32)  43.9 us
    dot_general x12, matrix products, newton_schulz(): jnp.dot(iterate, iterate.T, preferred_element_type=jnp.float32)  28.6 us
  transfers between devices with their start and end apart: 8, of which 7 were waited for; matrix products, arithmetic and copies ran while one was open for 6% of the time, Pallas kernels for 0%

profile of v1, /device:TPU:11, one launch (start us, length us, event | category | flops | bytes accessed | tf_op | source)
XLA Modules:
  0.0 511.6 jit_solution(1902232359138569491)
XLA Ops:
  20.5 63.5 %collective-permute-done.5 = f32[3,512,512]{1,2,0:T(8,128)S(1)} collective-permute-done((f32[3,512,512]{1,2,0:T(8,128)S(1)}, f32[3,512,512]{1,2,0:T(8,128)S(1)}, u32[]{:S(2)}, u32[]{:S(2)}) %collective-permute-start.5) | collective-permute-done | bytes 3145760 | tf_op jit(solution)/shard_map/ppermute | solution.py:61
  85.5 66.0 %collective-permute-done.1 = f32[3,512,512]{1,2,0:T(8,128)S(1)} collective-permute-done((f32[3,512,512]{1,2,0:T(8,128)S(1)}, f32[3,512,512]{1,2,0:T(8,128)S(1)}, u32[]{:S(2)}, u32[]{:S(2)}) %collective-permute-start.1) | collective-permute-done | bytes 3145760 | tf_op jit(solution)/shard_map/ppermute | solution.py:61
  157.6 126.1 %collective-permute-done.2 = f32[3,512,512]{1,2,0:T(8,128)S(1)} collective-permute-done((f32[3,512,512]{1,2,0:T(8,128)S(1)}, f32[3,512,512]{1,2,0:T(8,128)S(1)}, u32[]{:S(2)}, u32[]{:S(2)}) %collective-permute-start.2) | collective-permute-done | bytes 3145760 | tf_op jit(solution)/shard_map/ppermute | solution.py:61
  286.2 3.3 collective-permute-start.3
  289.5 2.8 copy.7
  292.3 3.0 fusion.60
  295.4 61.9 %collective-permute-done.7 = f32[3,512,512]{1,2,0:T(8,128)} collective-permute-done((f32[3,512,512]{1,2,0:T(8,128)}, f32[3,512,512]{1,2,0:T(8,128)}, u32[]{:S(2)}, u32[]{:S(2)}) %collective-permute-start.7) | collective-permute-done | bytes 3145760 | tf_op jit(solution)/shard_map/ppermute | solution.py:61
  357.3 3.4 add_convert_fusion
  363.7 3.5 fusion.33
  369.6 3.7 multiply_reduce_fusion.2
  373.3 51.5 %collective-permute-done.3 = f32[3,512,512]{1,2,0:T(8,128)} collective-permute-done((f32[3,512,512]{1,2,0:T(8,128)}, f32[3,512,512]{1,2,0:T(8,128)}, u32[]{:S(2)}, u32[]{:S(2)}) %collective-permute-start.3) | collective-permute-done | bytes 3145760 | tf_op jit(solution)/shard_map/ppermute | solution.py:61
  424.8 3.4 add_convert_fusion.1
  431.0 2.5 convolution_convert_fusion.7
  433.5 3.6 fusion.30
  437.1 2.5 convolution_convert_fusion.6
  439.6 3.6 multiply_reduce_fusion.3
  443.7 2.5 convolution_convert_fusion.3
  446.2 3.5 fusion.36
  452.2 4.2 multiply_reduce_fusion.1
  457.1 2.5 convolution_convert_fusion.1
  459.6 3.4 fusion.39
  465.5 4.2 multiply_reduce_fusion
  470.2 2.5 convolution_convert_fusion.11
  472.7 3.7 fusion.24
  476.4 2.5 convolution_convert_fusion.10
  478.9 3.6 multiply_reduce_fusion.5
  483.2 2.5 convolution_convert_fusion.9
  485.7 3.4 fusion.27
  489.1 2.5 convolution_convert_fusion.8
  491.6 3.6 multiply_reduce_fusion.4
  503.9 2.8 convolution_convert_fusion.12
  508.1 2.8 copy.10
  (76 shorter events, 52.2 us)
Async XLA Ops:
  0.6 6.3 %copy-start.7 = (bf16[128,1024]{1,0:T(8,128)(2,1)S(1)}, bf16[128,1024]{1,0:T(8,128)(2,1)}, u32[]{:S(2)}) copy-start(bf16[128,1024]{1,0:T(8,128)(2,1)} %param.5) | copy-start | bytes 786436
  7.6 1.9 copy-start
  7.6 2.1 copy-start.8
  7.9 6.0 %collective-permute-start.4 = (f32[3,512,512]{1,2,0:T(8,128)S(1)}, f32[3,512,512]{1,2,0:T(8,128)S(1)}, u32[]{:S(2)}, u32[]{:S(2)}) collective-permute-start(f32[3,512,512]{1,2,0:T(8,128)S(1)} %pad_maximum_fusion.1), channel_id=1, source_target_pairs={{0,1},{1,0},{2,3},{3,2},{4,5},{5,4},{6,7},{7,6},{8,9},{9,8},{10,11... | collective-permute-start | bytes 9437192 | tf_op jit(solution)/shard_map/ppermute | solution.py:61
  11.7 6.7 %collective-permute-start = (f32[3,512,512]{1,2,0:T(8,128)S(1)}, f32[3,512,512]{1,2,0:T(8,128)S(1)}, u32[]{:S(2)}, u32[]{:S(2)}) collective-permute-start(f32[3,512,512]{1,2,0:T(8,128)S(1)} %pad_maximum_fusion), channel_id=1, source_target_pairs={{0,1},{1,0},{2,3},{3,2},{4,5},{5,4},{6,7},{7,6},{8,9},{9,8},{10,11... | collective-permute-start | bytes 9437192 | tf_op jit(solution)/shard_map/ppermute | solution.py:61
  14.7 69.4 %collective-permute-start.5 = (f32[3,512,512]{1,2,0:T(8,128)S(1)}, f32[3,512,512]{1,2,0:T(8,128)S(1)}, u32[]{:S(2)}, u32[]{:S(2)}) collective-permute-start(f32[3,512,512]{1,2,0:T(8,128)S(1)} %fusion.220), channel_id=1, source_target_pairs={{0,2},{1,3},{2,0},{3,1},{4,6},{5,7},{6,4},{7,5},{8,10},{9,11},{10,... | collective-permute-start | bytes 9437192 | tf_op jit(solution)/shard_map/ppermute | solution.py:61
  19.2 132.3 %collective-permute-start.1 = (f32[3,512,512]{1,2,0:T(8,128)S(1)}, f32[3,512,512]{1,2,0:T(8,128)S(1)}, u32[]{:S(2)}, u32[]{:S(2)}) collective-permute-start(f32[3,512,512]{1,2,0:T(8,128)S(1)} %fusion.221), channel_id=1, source_target_pairs={{0,2},{1,3},{2,0},{3,1},{4,6},{5,7},{6,4},{7,5},{8,10},{9,11},{10,... | collective-permute-start | bytes 9437192 | tf_op jit(solution)/shard_map/ppermute | solution.py:61
  85.2 67.7 %collective-permute-start.6 = (f32[3,512,512]{1,2,0:T(8,128)S(1)}, f32[3,512,512]{1,2,0:T(8,128)S(1)}, u32[]{:S(2)}, u32[]{:S(2)}) collective-permute-start(f32[3,512,512]{1,2,0:T(8,128)S(1)} %fusion.265), channel_id=1, source_target_pairs={{0,4},{1,5},{2,6},{3,7},{4,0},{5,1},{6,2},{7,3},{8,12},{9,13},{10,... | collective-permute-start | bytes 9437192 | tf_op jit(solution)/shard_map/ppermute | solution.py:61
  152.7 131.1 %collective-permute-start.2 = (f32[3,512,512]{1,2,0:T(8,128)S(1)}, f32[3,512,512]{1,2,0:T(8,128)S(1)}, u32[]{:S(2)}, u32[]{:S(2)}) collective-permute-start(f32[3,512,512]{1,2,0:T(8,128)S(1)} %fusion.264), channel_id=1, source_target_pairs={{0,4},{1,5},{2,6},{3,7},{4,0},{5,1},{6,2},{7,3},{8,12},{9,13},{10,... | collective-permute-start | bytes 9437192 | tf_op jit(solution)/shard_map/ppermute | solution.py:61
  155.3 201.9 %collective-permute-start.7 = (f32[3,512,512]{1,2,0:T(8,128)}, f32[3,512,512]{1,2,0:T(8,128)}, u32[]{:S(2)}, u32[]{:S(2)}) collective-permute-start(f32[3,512,512]{1,2,0:T(8,128)} %add.261), channel_id=1, source_target_pairs={{0,8},{1,9},{2,10},{3,11},{4,12},{5,13},{6,14},{7,15},{8,0},{9,1},... | collective-permute-start | bytes 9437192 | tf_op jit(solution)/shard_map/ppermute | solution.py:61
  286.2 138.6 %collective-permute-start.3 = (f32[3,512,512]{1,2,0:T(8,128)}, f32[3,512,512]{1,2,0:T(8,128)}, u32[]{:S(2)}, u32[]{:S(2)}) collective-permute-start(f32[3,512,512]{1,2,0:T(8,128)} %add.233), channel_id=1, source_target_pairs={{0,8},{1,9},{2,10},{3,11},{4,12},{5,13},{6,14},{7,15},{8,0},{9,1},... | collective-permute-start | bytes 9437192 | tf_op jit(solution)/shard_map/ppermute | solution.py:61
  360.6 1.8 copy-start.3
  363.7 5.9 %copy-start.1 = (bf16[2,3,512,512]{2,3,1,0:T(8,128)(2,1)S(1)}, bf16[2,3,512,512]{2,3,1,0:T(8,128)(2,1)}, u32[]{:S(2)}) copy-start(bf16[2,3,512,512]{2,3,1,0:T(8,128)(2,1)} %copy.7) | copy-start | bytes 9437188
  428.2 1.2 copy-start.2
  495.2 3.0 copy-start.5
  500.5 3.1 copy-start.6
  500.5 3.2 copy-start.10
  500.5 3.2 copy-start.11
  500.5 3.2 copy-start.12
  500.5 3.2 copy-start.4
  508.1 2.8 copy-start.9
